TPU v7x, 256 devices: a whole 4x4x8 slice. The times are simulated.
256 devices in a mesh: tgt: 4 (over z_lo, core), sup: 64 (over y, x, z_hi).
Axes of the slice: x: 4, y: 4, z: 8 (z_hi: 4, z_lo: 2; z = z_hi * 2 + z_lo), core: 2. Of those that a mesh axis runs over, the one named last changes fastest.
Arguments:
- support_images: bfloat16 [512, 3072], P('sup'), may hold values from -6 to 6
- target_images: bfloat16 [262144, 3072], P(('tgt', 'sup')), may hold values from -6 to 6
- support_labels: int32 [512], replicated, may hold values from 0 to 99
- target_labels: int32 [262144], P(('tgt', 'sup')), may hold values from 0 to 99
Outputs:
- scaled_grad: float32 [512, 3072], P('sup')
- loss: float32 [], replicated
All inputs are finite; a program needn't handle non-finite values.
Results may differ from a plain program's by a relative error of at most 0.0095.
Values may be sent and summed in bfloat16 or wider, within the bound.
A program may use at most 128 MiB of HBM per device.

v0:
```python
import math
import jax
import jax.numpy as jnp
from jax import lax
from jax.sharding import PartitionSpec as P

D = 3072
C = 100
LAYERS = 5
ridge_scale = 0.1
two_over_pi = 2.0 / math.pi


def ntk_kernel(gram_in, norm_row, norm_col):
    tangent = gram_in
    for layer_no in range(LAYERS):
        spread = (1.0 + 2.0 * norm_row) * (1.0 + 2.0 * norm_col)
        new_gram = two_over_pi * jnp.arcsin(2.0 * gram_in / jnp.sqrt(spread))
        slope_term = 2.0 * two_over_pi / jnp.sqrt(spread - 4.0 * gram_in * gram_in)
        tangent = new_gram + tangent * slope_term
        norm_row = two_over_pi * jnp.arcsin(2.0 * norm_row / (1.0 + 2.0 * norm_row))
        norm_col = two_over_pi * jnp.arcsin(2.0 * norm_col / (1.0 + 2.0 * norm_col))
        gram_in = new_gram
    return tangent


def ridge_solve(factor, rhs_block):
    middle = lax.linalg.triangular_solve(factor, rhs_block, left_side=True, lower=True)
    return lax.linalg.triangular_solve(factor, middle, left_side=True, lower=True, transpose_a=True)


def make_terms(
    coef_ts, coef_ss, target_images, support_images, rows_sup, column_scale, first_group
):
    back_dims = (((0,), (0,)), ((), ()))

    def term_rows(start, row_count):
        result = lax.dot_general(
            coef_ts, target_images, back_dims, preferred_element_type=jnp.float32
        )
        result = result + first_group * lax.dot_general(
            coef_ss, support_images, back_dims, preferred_element_type=jnp.float32
        )
        return result + column_scale[:, None] * rows_sup.astype(jnp.float32)

    return term_rows


def body(support_images, target_images, support_labels, target_labels):
    sup_rows = support_images.shape[0]
    tgt_rows = target_images.shape[0]
    n_sup = lax.axis_size("sup")
    n_tgt = lax.axis_size("tgt")
    total_sup = sup_rows * n_sup
    total_tgt = tgt_rows * n_sup * n_tgt
    contract = (((1,), (1,)), ((), ()))
    gathered = lax.all_gather(support_images, "sup", axis=0, tiled=True)
    norm_all = jnp.sum(jnp.square(gathered.astype(jnp.float32)), axis=1) / D
    norm_own = jnp.sum(jnp.square(support_images.astype(jnp.float32)), axis=1) / D
    norm_tgt = jnp.sum(jnp.square(target_images.astype(jnp.float32)), axis=1) / D
    gram_ts = (
        lax.dot_general(target_images, gathered, contract, preferred_element_type=jnp.float32) / D
    )
    gram_ss = (
        lax.dot_general(support_images, gathered, contract, preferred_element_type=jnp.float32) / D
    )
    kern_ts, pull_ts = jax.vjp(ntk_kernel, gram_ts, norm_tgt[:, None], norm_all[None, :])
    kern_own, pull_ss = jax.vjp(ntk_kernel, gram_ss, norm_own[:, None], norm_all[None, :])
    kern_ss = lax.all_gather(kern_own, "sup", axis=0, tiled=True)
    trace_mean = jnp.trace(kern_ss) / total_sup
    system = kern_ss + ridge_scale * trace_mean * jnp.eye(total_sup, dtype=jnp.float32)
    factor = jnp.linalg.cholesky(system)
    classes = jnp.arange(C, dtype=jnp.int32)
    label_sup = (support_labels[:, None] == classes[None, :]).astype(jnp.float32) - 1.0 / C
    label_tgt = (target_labels[:, None] == classes[None, :]).astype(jnp.float32) - 1.0 / C
    coeffs = ridge_solve(factor, label_sup)
    misfit = jnp.dot(kern_ts, coeffs, precision=lax.Precision.HIGHEST) - label_tgt
    loss_part = jnp.sum(misfit * misfit) / (2.0 * total_tgt)
    d_predict = misfit / total_tgt
    d_coeff_part = jnp.dot(kern_ts.T, d_predict, precision=lax.Precision.HIGHEST)
    d_coeffs, loss_value = lax.psum((d_coeff_part, loss_part), ("tgt", "sup"))
    adjoint = ridge_solve(factor, d_coeffs)
    ridge_grad = -ridge_scale / total_sup * jnp.sum(adjoint * coeffs)
    start_own = lax.axis_index("sup") * sup_rows
    adjoint_own = lax.dynamic_slice_in_dim(adjoint, start_own, sup_rows, 0)
    row_ids = start_own + jnp.arange(sup_rows, dtype=jnp.int32)
    col_ids = jnp.arange(total_sup, dtype=jnp.int32)
    diagonal = (row_ids[:, None] == col_ids[None, :]).astype(jnp.float32)
    d_kern_own = (
        -jnp.dot(adjoint_own, coeffs.T, precision=lax.Precision.HIGHEST) + ridge_grad * diagonal
    )
    d_kern_ts = jnp.dot(d_predict, coeffs.T, precision=lax.Precision.HIGHEST)
    g_ts, unused_tgt, qcol_ts = pull_ts(d_kern_ts)
    g_ss, qrow_ss, qcol_ss = pull_ss(d_kern_own)
    first_group = (lax.axis_index("tgt") == 0).astype(jnp.float32)
    coef_ts = (g_ts / D).astype(jnp.bfloat16)
    coef_ss = (g_ss / D).astype(jnp.bfloat16)
    column_scale = 2.0 / D * (qcol_ts[0] + first_group * qcol_ss[0])
    term_rows = make_terms(
        coef_ts, coef_ss, target_images, support_images, gathered, column_scale, first_group
    )
    partial_rows = lax.psum_scatter(
        term_rows(jnp.int32(0), sup_rows * lax.axis_size("sup")),
        "sup",
        scatter_dimension=0,
        tiled=True,
    )
    summed = lax.psum(partial_rows, "tgt")
    local_rows = jnp.dot(coef_ss, gathered, preferred_element_type=jnp.float32)
    local_rows = local_rows + 2.0 / D * qrow_ss * support_images.astype(jnp.float32)
    return (total_sup * (summed + local_rows), loss_value)


def solution(mesh):
    in_specs = (P("sup", None), P(("tgt", "sup"), None), P(), P(("tgt", "sup")))
    out_specs = (P("sup", None), P())
    return jax.shard_map(body, mesh=mesh, in_specs=in_specs, out_specs=out_specs, check_vma=False)
```

profile of v0, /device:TPU:1, one launch (start us, length us, event | category | flops | bytes accessed | tf_op | source)
XLA Modules:
  0.0 937.1 jit_solution(4720406489037573649)
XLA Ops:
  10.6 4.1 multiply_reduce_fusion
  15.8 82.0 %all-gather.3.cloned.1.call-done = bf16[512,3072]{1,0:T(8,128)(2,1)} async-done(((bf16[8,3072]{1,0:T(8,128)(2,1)}), bf16[512,3072]{1,0:T(8,128)(2,1)}) %all-gather.3.cloned.1.call-update) | async-done | bytes 3145744 | tf_op jit(solution)/shard_map/all_gather | solution.py:57
  97.8 2.7 fusion
  101.4 1.8 multiply_add_fusion.5
  103.5 36.9 %multiply_add_fusion = (f32[1024,512]{1,0:T(8,128)}, f32[1024,512]{1,0:T(8,128)}, f32[1024,512]{1,0:T(8,128)}, f32[1024,512]{1,0:T(8,128)}) fusion(f32[512]{0:T(512)S(1)} %get-tuple-element.154, f32[1024]{0:T(1024)S(1)} %multiply_add_fusion.10, f32[512]{0:T(512)S(1)} %get-tuple-element.119, f32[1024]{0:T(1024)S(1)} %get-tuple-element.135, ...), kind=kOutput, calls=%fused_computation.109 | convolution fusion | flops 3261071360 | bytes 17856512 | tf_op jit(solution)/shard_map/dot_general | solution.py:62
  140.5 35.2 %all-gather.5.cloned.1.call-done = f32[512,512]{1,0:T(8,128)} async-done(((f32[8,512]{1,0:T(8,128)}), f32[512,512]{1,0:T(8,128)}) %all-gather.5.cloned.1.call-update) | async-done | bytes 1048592 | tf_op jit(solution)/shard_map/all_gather | solution.py:69
  175.7 2.5 copy.23
  178.2 1.9 select_reduce_fusion
  180.8 2.3 select_add_fusion
  183.1 2.6 copy.24
  185.7 1.8 fusion.99
  187.5 1.0 copy-done.3
  188.5 11.7 %cholesky.103 = f32[128,128]{1,0:T(8,128)S(1)} custom-call(f32[128,128]{1,0:T(8,128)S(1)} %cholesky.263), custom_call_target="Cholesky" | custom-call | tf_op jit(solution)/shard_map/jit(cholesky)/cholesky | solution.py:72
  200.9 9.8 %custom-call.33 = f32[1,128,128]{1,2,0:T(8,128)S(1)} custom-call(f32[1,128,128]{2,1,0:T(8,128)S(1)} %get-tuple-element.131), custom_call_target="InvertDiagBlocksLowerTriangular" | custom-call | tf_op jit(solution)/shard_map/jit(cholesky)/cholesky | solution.py:72
  210.7 1.2 fusion.110
  211.9 1.3 convolution_subtract_fusion.1
  213.9 11.7 %cholesky.215 = f32[128,128]{1,0:T(8,128)S(1)} custom-call(f32[128,128]{1,0:T(8,128)S(1)} %cholesky.267), custom_call_target="Cholesky" | custom-call | tf_op jit(solution)/shard_map/jit(cholesky)/cholesky | solution.py:72
  225.6 1.2 select_reduce_fusion.3
  228.6 1.1 cholesky.222
  229.6 11.0 %custom-call.34 = f32[1,128,128]{1,2,0:T(8,128)S(1)} custom-call(f32[1,128,128]{2,1,0:T(8,128)} %get-tuple-element.129), custom_call_target="InvertDiagBlocksLowerTriangular" | custom-call | tf_op jit(solution)/shard_map/jit(cholesky)/cholesky | solution.py:72
  241.4 1.5 constant_dynamic-update-slice_fusion.2
  242.8 1.9 convolution_dynamic-update-slice_fusion
  244.7 1.6 convolution_subtract_fusion.2
  246.4 11.7 %cholesky.236 = f32[128,128]{1,0:T(8,128)S(1)} custom-call(f32[128,128]{1,0:T(8,128)S(1)} %cholesky.272), custom_call_target="Cholesky" | custom-call | tf_op jit(solution)/shard_map/jit(cholesky)/cholesky | solution.py:72
  258.9 9.8 %custom-call.35 = f32[1,128,128]{1,2,0:T(8,128)S(1)} custom-call(f32[1,128,128]{2,1,0:T(8,128)S(1)} %get-tuple-element.127), custom_call_target="InvertDiagBlocksLowerTriangular" | custom-call | tf_op jit(solution)/shard_map/jit(cholesky)/cholesky | solution.py:72
  269.6 1.5 convolution_subtract_fusion.6
  271.1 11.9 %cholesky.253 = f32[128,128]{1,0:T(8,128)S(1)} custom-call(f32[128,128]{1,0:T(8,128)S(1)} %convolution_subtract_fusion.6), custom_call_target="Cholesky" | custom-call | tf_op jit(solution)/shard_map/jit(cholesky)/cholesky | solution.py:72
  288.9 2.4 select_select_fusion
  291.3 14.5 %while.8 = (s32[]{:T(128)}, f32[512,512]{0,1:T(8,128)}, s32[4,2]{0,1:T(2,128)S(1)}, f32[4,128,128]{2,1,0:T(8,128)}, s32[]{:T(128)}) while((s32[]{:T(128)}, f32[512,512]{0,1:T(8,128)}, s32[4,2]{0,1:T(2,128)S(1)}, f32[4,128,128]{2,1,0:T(8,128)}, s32[]{:T(128)}) %tuple.98), condition=%wide.while_cond.1, body=%wide.while_body.1.sunk | while | flops 2 | bytes 393829 | solution.py:29
  291.9 2.3 dynamic-slice.14
  295.6 2.3 dynamic-slice.14
  299.2 2.3 dynamic-slice.14
  302.8 2.2 dynamic-slice.14
  305.7 40.1 %custom-call.39 = f32[4,128,128]{1,2,0:T(8,128)S(1)} custom-call(f32[4,128,128]{2,1,0:T(8,128)} %get-tuple-element.33), custom_call_target="InvertDiagBlocksLowerTriangular" | custom-call | tf_op jit(solution)/shard_map/triangular_solve/custom-call.8 | solution.py:29
  345.9 1.3 fusion.155
  347.2 1.2 convolution_subtract_fusion.4
  348.6 1.3 convolution_subtract_fusion.3
  350.2 1.4 convolution_subtract_fusion.5
  352.2 1.1 convolution_subtract_fusion.12
  353.6 1.2 convolution_subtract_fusion.11
  355.0 1.3 convolution_subtract_fusion.15
  356.7 2.8 multiply_reduce_fusion.1
  360.2 2.1 fusion.102
  362.5 18.7 %fusion.81 = (f32[1024,512]{1,0:T(8,128)S(1)}, f32[1024,512]{1,0:T(8,128)S(1)}, f32[1024,512]{1,0:T(8,128)S(1)}) fusion(f32[512]{0:T(512)} %copy-done.32, f32[1024]{0:T(1024)} %copy-done.50, f32[512]{0:T(512)S(1)} %copy-done.20, f32[1024]{0:T(1024)} %copy-done.38, f32[1024,512]{1,0:T(8,128)} %get-tuple-element.115, f32[512]{0:T(512)S(1)} %copy-done.22, ...), kind=kOutput, calls=%fused_computation.97 | convolution fusion | flops 658761728 | bytes 11118592 | tf_op jit(solution)/shard_map/dot_general | solution.py:92
  381.3 26.9 %fusion.92 = (f32[512]{0:T(512)}, f32[512]{0:T(512)}, f32[512]{0:T(512)}, f32[1024,512]{1,0:T(8,128)S(1)}, f32[1024,512]{1,0:T(8,128)S(1)}) fusion(f32[512]{0:T(512)S(1)} %copy-done.33, f32[1024]{0:T(1024)S(1)} %copy-done.51, f32[1024,512]{1,0:T(8,128)S(1)} %get-tuple-element.151, f32[1024,512]{1,0:T(8,128)S(1)} %copy-done.58, f32[512]{0:T(512)S(1)} %copy-done.20, ...), kind=kLoop, calls=%fused_computation.128 | loop fusion | flops 67107328 | bytes 16814080 | tf_op jit(solution)/shard_map/transpose(jvp())/reduce_sum | solution.py:17
  408.2 14.4 %fusion.61 = (f32[1024,512]{1,0:T(8,128)S(1)}, f32[1024,512]{1,0:T(8,128)S(1)}) fusion(f32[1024,512]{1,0:T(8,128)S(1)} %get-tuple-element.92, f32[1024,512]{1,0:T(8,128)S(1)} %get-tuple-element.91, f32[1024,512]{1,0:T(8,128)S(1)} %copy-done.4, f32[512]{0:T(512)S(1)} %copy-done.22, f32[1024]{0:T(1024)S(1)} %copy-done.37, f32[512]{0:T(512)S(1)} %copy-done.17, ...), kind=kLoop, calls=%fused_computation.77 | loop fusion | flops 24117248 | bytes 14704640 | tf_op jit(solution)/shard_map/transpose(jvp())/mul | solution.py:18
  422.6 12.5 %fusion.89 = (f32[512]{0:T(512)}, f32[512]{0:T(512)}, f32[1024,512]{1,0:T(8,128)S(1)}) fusion(f32[1024,512]{1,0:T(8,128)S(1)} %get-tuple-element.103, f32[512]{0:T(512)S(1)} %copy-done.17, f32[1024]{0:T(1024)S(1)} %copy-done.26, f32[1024,512]{1,0:T(8,128)S(1)} %get-tuple-element.104, f32[1024,512]{1,0:T(8,128)S(1)} %copy-done.2, f32[512]{0:T(512)S(1)} %copy-done.15, ...), kind=kLoop, calls=%fused_computation.125 | loop fusion | flops 36699136 | bytes 8404992 | tf_op jit(solution)/shard_map/transpose(jvp())/reduce_sum | solution.py:17
  435.1 14.1 %fusion.100 = f32[512,3072]{1,0:T(8,128)} fusion(bf16[1024,3072]{1,0:T(8,128)(2,1)S(1)} %bitcast.103, f32[1024,512]{1,0:T(8,128)S(1)} %get-tuple-element.93, f32[1024,512]{1,0:T(8,128)S(1)} %copy-done.2, f32[512]{0:T(512)S(1)} %copy-done.15, f32[1024]{0:T(1024)S(1)} %copy-done.24, f32[1024,512]{1,0:T(8,128)S(1)} %get-tuple-element.104, ...), kind=kOutput, calls=%fused_computation.161 | convolution fusion | flops 3242196992 | bytes 18886656 | tf_op jit(solution)/shard_map/dot_general | solution.py:38
  449.1 157.9 %all-reduce.4.cloned.1.call-done = f32[512,100]{0,1:T(8,128)} async-done(((f32[512,100]{0,1:T(8,128)}), f32[512,100]{0,1:T(8,128)}) %all-reduce.4.cloned.1.call-update) | async-done | bytes 204816 | tf_op jit(solution)/shard_map/psum | solution.py:81
  607.0 1.1 fusion.166
  608.1 1.1 convolution_subtract_fusion.10
  609.4 1.2 convolution_subtract_fusion.9
  611.0 1.3 convolution_subtract_fusion.14
  612.8 1.1 convolution_subtract_fusion.8
  614.2 1.2 convolution_subtract_fusion.7
  615.6 1.3 convolution_subtract_fusion.13
  618.6 1.3 fusion.209
  619.9 1.1 multiply_reduce_fusion.6
  621.0 1.1 multiply_reduce_fusion.5
  625.4 6.9 fusion.1
  633.1 78.1 %psum.23 = f32[]{:T(128)} all-reduce(f32[]{:T(128)S(6)} %div.757), channel_id=1, replica_groups=mesh['tgt'=4,'sup'=64] {'tgt','sup'}, use_global_device_ids=true, to_apply=%region_32.35 | all-reduce | flops 1 | bytes 8 | tf_op jit(solution)/shard_map/psum | solution.py:81
  711.2 174.7 %reduce-scatter.2.cloned.1.call-done = f32[8,3072]{1,0:T(8,128)} async-done(((f32[512,3072]{1,0:T(8,128)}), f32[8,3072]{1,0:T(8,128)}) %reduce-scatter.2.cloned.1.call-update) | async-done | bytes 98320 | tf_op jit(solution)/shard_map/reduce_scatter | solution.py:102
  886.0 42.1 %all-reduce.6.cloned.1.call-done = f32[8,3072]{1,0:T(8,128)} async-done(((f32[8,3072]{1,0:T(8,128)}), f32[8,3072]{1,0:T(8,128)}) %all-reduce.6.cloned.1.call-update) | async-done | bytes 98320 | tf_op jit(solution)/shard_map/psum | solution.py:108
  928.1 2.2 fusion.3
  (200 shorter events, 28.6 us)
Async XLA Ops:
  7.2 90.6 %all-gather.3.cloned.1.call-start = ((), (), s32[]{:S(2)}) async-start(), calls=%async_computation.1 | async-start | bytes 3194880 | tf_op jit(solution)/shard_map/all_gather | solution.py:57
  7.9 167.8 %all-gather.5.cloned.1.call-start = ((), (), s32[]{:S(2)}) async-start(), calls=%async_computation.2 | async-start | bytes 1064960 | tf_op jit(solution)/shard_map/all_gather | solution.py:69
  9.9 0.5 copy-start.42
  10.1 4.6 copy-start.53
  10.1 91.2 %copy-start.27 = (f32[8]{0:T(128)}, f32[8]{0:T(128)S(1)}, u32[]{:S(2)}) copy-start(f32[8]{0:T(128)S(1)} %get-tuple-element.148) | copy-start | bytes 100
  10.1 91.2 %copy-start.40 = (f32[8]{0:T(128)}, f32[8]{0:T(128)S(1)}, u32[]{:S(2)}) copy-start(f32[8]{0:T(128)S(1)} %get-tuple-element.110) | copy-start | bytes 100
  10.1 91.2 %copy-start.34 = (f32[8]{0:T(128)}, f32[8]{0:T(128)S(1)}, u32[]{:S(2)}) copy-start(f32[8]{0:T(128)S(1)} %broadcast_add_fusion.8) | copy-start | bytes 100
  10.6 90.7 %copy-start.41 = (f32[8]{0:T(128)}, f32[8]{0:T(128)S(1)}, u32[]{:S(2)}) copy-start(f32[8]{0:T(128)S(1)} %get-tuple-element.156) | copy-start | bytes 100
  10.6 90.7 %copy-start.48 = (f32[8]{0:T(128)}, f32[8]{0:T(128)S(1)}, u32[]{:S(2)}) copy-start(f32[8]{0:T(128)S(1)} %get-tuple-element.155) | copy-start | bytes 100
  10.6 4.4 copy-start.52
  14.7 86.6 %copy-start.6 = (bf16[8,3072]{1,0:T(8,128)(2,1)S(1)}, bf16[8,3072]{1,0:T(8,128)(2,1)}, u32[]{:S(2)}) copy-start(bf16[8,3072]{1,0:T(8,128)(2,1)} %param.8) | copy-start | bytes 147460
  14.9 88.5 %copy-start.23 = (f32[1024]{0:T(1024)}, f32[1024]{0:T(1024)S(1)}, u32[]{:S(2)}) copy-start(f32[1024]{0:T(1024)S(1)} %get-tuple-element.133) | copy-start | bytes 12292
  14.9 88.5 %copy-start.25 = (f32[1024]{0:T(1024)}, f32[1024]{0:T(1024)S(1)}, u32[]{:S(2)}) copy-start(f32[1024]{0:T(1024)S(1)} %get-tuple-element.137) | copy-start | bytes 12292
  14.9 88.5 %copy-start.36 = (f32[1024]{0:T(1024)}, f32[1024]{0:T(1024)S(1)}, u32[]{:S(2)}) copy-start(f32[1024]{0:T(1024)S(1)} %get-tuple-element.134) | copy-start | bytes 12292
  14.9 88.5 %copy-start.38 = (f32[1024]{0:T(1024)}, f32[1024]{0:T(1024)S(1)}, u32[]{:S(2)}) copy-start(f32[1024]{0:T(1024)S(1)} %get-tuple-element.135) | copy-start | bytes 12292
  15.0 88.5 %copy-start.50 = (f32[1024]{0:T(1024)}, f32[1024]{0:T(1024)S(1)}, u32[]{:S(2)}) copy-start(f32[1024]{0:T(1024)S(1)} %multiply_add_fusion.10) | copy-start | bytes 12292
  97.8 3.6 copy-start
  100.5 0.6 copy-start.31
  100.7 0.6 copy-start.29
  100.7 0.6 copy-start.30
  100.7 39.7 %copy-start.14 = (f32[512]{0:T(512)}, f32[512]{0:T(512)S(1)}, u32[]{:S(2)}) copy-start(f32[512]{0:T(512)S(1)} %get-tuple-element.145) | copy-start | bytes 6148
  100.7 39.7 %copy-start.19 = (f32[512]{0:T(512)}, f32[512]{0:T(512)S(1)}, u32[]{:S(2)}) copy-start(f32[512]{0:T(512)S(1)} %get-tuple-element.119) | copy-start | bytes 6148
  101.2 39.3 %copy-start.16 = (f32[512]{0:T(512)}, f32[512]{0:T(512)S(1)}, u32[]{:S(2)}) copy-start(f32[512]{0:T(512)S(1)} %get-tuple-element.146) | copy-start | bytes 6148
  101.2 39.3 %copy-start.21 = (f32[512]{0:T(512)}, f32[512]{0:T(512)S(1)}, u32[]{:S(2)}) copy-start(f32[512]{0:T(512)S(1)} %get-tuple-element.147) | copy-start | bytes 6148
  101.2 39.3 %copy-start.32 = (f32[512]{0:T(512)}, f32[512]{0:T(512)S(1)}, u32[]{:S(2)}) copy-start(f32[512]{0:T(512)S(1)} %get-tuple-element.154) | copy-start | bytes 6148
  103.2 503.8 %all-reduce.4.cloned.1.call-start = ((), (), s32[]{:S(2)}) async-start(), calls=%async_computation.3 | async-start | bytes 425984 | tf_op jit(solution)/shard_map/psum | solution.py:81
  187.5 1.1 copy-start.3
  200.2 0.6 copy-start.13
  213.2 0.7 copy-start.10
  241.3 41.8 %copy-start.56 = (f32[128]{0:T(128)S(1)}, f32[128]{0:T(128)}, u32[]{:S(2)}) copy-start(f32[128]{0:T(128)} %get-tuple-element.128) | copy-start | bytes 1540
  241.3 42.5 %copy-start.55 = (f32[128]{0:T(128)S(1)}, f32[128]{0:T(128)}, u32[]{:S(2)}) copy-start(f32[128]{0:T(128)} %get-tuple-element.130) | copy-start | bytes 1540
  244.7 46.6 %copy-start.57 = (s32[4]{0:T(128)S(1)}, s32[4]{0:T(128)}, u32[]{:S(2)}) copy-start(s32[4]{0:T(128)} %iota_multiply_fusion) | copy-start | bytes 52
  305.7 50.9 %copy-start.49 = (s32[1024]{0:T(1024)S(1)}, s32[1024]{0:T(1024)}, u32[]{:S(2)}) copy-start(s32[1024]{0:T(1024)} %param.11) | copy-start | bytes 12292
  345.9 10.8 %copy-start.1 = (f32[1024,512]{1,0:T(8,128)S(1)}, f32[1024,512]{1,0:T(8,128)}, u32[]{:S(2)}) copy-start(f32[1024,512]{1,0:T(8,128)} %get-tuple-element.114) | copy-start | bytes 6291460
  355.0 1.6 copy-start.8
  356.6 2.9 copy-start.11
  359.5 0.8 copy-start.5
  359.5 2.9 copy-start.20
  359.5 2.9 copy-start.22
  362.3 523.6 %reduce-scatter.2.cloned.1.call-start = ((), (), s32[]{:S(2)}) async-start(), calls=%async_computation.4 | async-start | bytes 6389760 | tf_op jit(solution)/shard_map/reduce_scatter | solution.py:102
  362.4 18.8 %copy-start.2 = (f32[1024,512]{1,0:T(8,128)S(1)}, f32[1024,512]{1,0:T(8,128)}, u32[]{:S(2)}) copy-start(f32[1024,512]{1,0:T(8,128)} %get-tuple-element.149) | copy-start | bytes 6291460
  362.4 18.8 %copy-start.4 = (f32[1024,512]{1,0:T(8,128)S(1)}, f32[1024,512]{1,0:T(8,128)}, u32[]{:S(2)}) copy-start(f32[1024,512]{1,0:T(8,128)} %get-tuple-element.116) | copy-start | bytes 6291460
  362.4 18.8 %copy-start.15 = (f32[512]{0:T(512)S(1)}, f32[512]{0:T(512)}, u32[]{:S(2)}) copy-start(f32[512]{0:T(512)} %copy-done.14) | copy-start | bytes 6148
  362.4 18.8 %copy-start.17 = (f32[512]{0:T(512)S(1)}, f32[512]{0:T(512)}, u32[]{:S(2)}) copy-start(f32[512]{0:T(512)} %copy-done.16) | copy-start | bytes 6148
  362.4 18.8 %copy-start.24 = (f32[1024]{0:T(1024)S(1)}, f32[1024]{0:T(1024)}, u32[]{:S(2)}) copy-start(f32[1024]{0:T(1024)} %copy-done.23) | copy-start | bytes 12292
  362.5 18.8 %copy-start.26 = (f32[1024]{0:T(1024)S(1)}, f32[1024]{0:T(1024)}, u32[]{:S(2)}) copy-start(f32[1024]{0:T(1024)} %copy-done.25) | copy-start | bytes 12292
  362.5 18.8 %copy-start.33 = (f32[512]{0:T(512)S(1)}, f32[512]{0:T(512)}, u32[]{:S(2)}) copy-start(f32[512]{0:T(512)} %copy-done.32) | copy-start | bytes 6148
  362.5 18.8 %copy-start.37 = (f32[1024]{0:T(1024)S(1)}, f32[1024]{0:T(1024)}, u32[]{:S(2)}) copy-start(f32[1024]{0:T(1024)} %copy-done.36) | copy-start | bytes 12292
  362.5 18.8 %copy-start.39 = (f32[1024]{0:T(1024)S(1)}, f32[1024]{0:T(1024)}, u32[]{:S(2)}) copy-start(f32[1024]{0:T(1024)} %copy-done.38) | copy-start | bytes 12292
  362.5 18.8 %copy-start.51 = (f32[1024]{0:T(1024)S(1)}, f32[1024]{0:T(1024)}, u32[]{:S(2)}) copy-start(f32[1024]{0:T(1024)} %copy-done.50) | copy-start | bytes 12292
  362.5 18.8 %copy-start.58 = (f32[1024,512]{1,0:T(8,128)S(1)}, f32[1024,512]{1,0:T(8,128)}, u32[]{:S(2)}) copy-start(f32[1024,512]{1,0:T(8,128)} %get-tuple-element.115) | copy-start | bytes 6291460
  381.3 53.8 %slice-start = ((s8[6291456]{0:T(1024)(128)(4,1)}), s8[4194304]{0:T(1024)(128)(4,1)S(1)}, s32[]{:S(2)}) async-start(s8[6291456]{0:T(1024)(128)(4,1)} %bitcast.102), calls=%async_computation.6 | async-start | bytes 8388608
  408.2 26.8 %slice-start.1 = ((s8[6291456]{0:T(1024)(128)(4,1)}), s8[2097152]{0:T(1024)(128)(4,1)S(1)}, s32[]{:S(2)}) async-start(s8[6291456]{0:T(1024)(128)(4,1)} %bitcast.102), calls=%async_computation.7 | async-start | bytes 4194304
  449.1 169.5 %copy-start.18 = (f32[8,512]{1,0:T(8,128)S(1)}, f32[8,512]{1,0:T(8,128)}, u32[]{:S(2)}) copy-start(f32[8,512]{1,0:T(8,128)} %get-tuple-element.109) | copy-start | bytes 49156
  607.0 10.2 %copy-start.9 = (f32[128,100]{0,1:T(8,128)S(1)}, f32[128,100]{0,1:T(8,128)}, u32[]{:S(2)}) copy-start(f32[128,100]{0,1:T(8,128)} %copy-done.8) | copy-start | bytes 153604
  607.0 10.2 %copy-start.12 = (f32[128,100]{0,1:T(8,128)S(1)}, f32[128,100]{0,1:T(8,128)}, u32[]{:S(2)}) copy-start(f32[128,100]{0,1:T(8,128)} %copy-done.11) | copy-start | bytes 153604
  632.4 253.6 %copy-start.43 = (f32[8]{0:T(128)S(1)}, f32[8]{0:T(128)}, u32[]{:S(2)}) copy-start(f32[8]{0:T(128)} %copy-done.42) | copy-start | bytes 100
  632.4 253.6 %copy-start.45 = (f32[8]{0:T(128)S(1)}, f32[8]{0:T(128)}, u32[]{:S(2)}) copy-start(f32[8]{0:T(128)} %copy-done.44) | copy-start | bytes 100
  632.4 253.6 %copy-start.47 = (f32[8]{0:T(128)S(1)}, f32[8]{0:T(128)}, u32[]{:S(2)}) copy-start(f32[8]{0:T(128)} %copy-done.46) | copy-start | bytes 100
  632.4 253.6 %copy-start.54 = (f32[8]{0:T(128)S(1)}, f32[8]{0:T(128)}, u32[]{:S(2)}) copy-start(f32[8]{0:T(128)} %copy-done.53) | copy-start | bytes 100
  632.4 295.8 %copy-start.7 = (bf16[8,3072]{1,0:T(8,128)(2,1)S(1)}, bf16[8,3072]{1,0:T(8,128)(2,1)}, u32[]{:S(2)}) copy-start(bf16[8,3072]{1,0:T(8,128)(2,1)} %param.8) | copy-start | bytes 147460
  632.4 295.8 %copy-start.28 = (f32[8]{0:T(128)S(1)}, f32[8]{0:T(128)}, u32[]{:S(2)}) copy-start(f32[8]{0:T(128)} %copy-done.27) | copy-start | bytes 100
  632.4 295.7 %copy-start.35 = (f32[8]{0:T(128)S(1)}, f32[8]{0:T(128)}, u32[]{:S(2)}) copy-start(f32[8]{0:T(128)} %copy-done.34) | copy-start | bytes 100
  632.4 295.7 %all-reduce.6.cloned.1.call-start = ((), (), s32[]{:S(2)}) async-start(), calls=%async_computation.5 | async-start | bytes 196608 | tf_op jit(solution)/shard_map/psum | solution.py:108
  (2 other events, 1.0 us)
Sparse Core Ops, SparseCore 0:
  11.3 86.4 all-gather.2
  103.3 72.3 all-gather.4
  362.5 244.4 all-reduce.3
  632.5 253.3 reduce-scatter.1
  888.5 39.5 all-reduce.5
where the time goes:
time: 942 us; the launch traced here: 937 us
  waiting for transfers between devices  493 us (52%)
  other arithmetic  201 us (21%)
  matrix products  116 us (12%)
  blocking collectives  78.1 us (8%)
  local copies, waits for them, and re-layouts  29.7 us (3%)
  between operations  19.5 us (2%)
    reduce_scatter x1, waiting for transfers between devices, body(): lax.psum_scatter(term_rows(jnp.int32(0), sup_rows * lax.axis_size('sup'))...  175 us
    psum x1, waiting for transfers between devices, body(): d_coeffs, loss_value = lax.psum((d_coeff_part, loss_part), ('tgt', 'sup'))  158 us
    another operation x15, other arithmetic, body(): factor = jnp.linalg.cholesky(system)  82 us
    all_gather x1, waiting for transfers between devices, body(): gathered = lax.all_gather(support_images, 'sup', axis=0, tiled=True)  82 us
    psum x1, blocking collectives, body(): d_coeffs, loss_value = lax.psum((d_coeff_part, loss_part), ('tgt', 'sup'))  78.1 us
    reduce_sum x7, other arithmetic, ntk_kernel(): spread = (1.0 + 2.0 * norm_row) * (1.0 + 2.0 * norm_col)  44.1 us
    another operation x4, other arithmetic, ridge_solve(): lax.linalg.triangular_solve(factor, middle, left_side=True, lower=True, t...  43.1 us
    psum x1, waiting for transfers between devices, body(): summed = lax.psum(partial_rows, 'tgt')  42.1 us
  transfers between devices with their start and end apart: 5, of which 5 were waited for; matrix products, arithmetic and copies ran while one was open for 14% of the time, Pallas kernels for 0%

commit v1 on v0

--- a/solution.py
+++ b/solution.py
@@ -105,7 +105,8 @@
         scatter_dimension=0,
         tiled=True,
     )
-    summed = lax.psum(partial_rows, "tgt")
+    blocks = lax.all_gather(partial_rows, "tgt", axis=0, tiled=False)
+    summed = blocks.sum(axis=0)
     local_rows = jnp.dot(coef_ss, gathered, preferred_element_type=jnp.float32)
     local_rows = local_rows + 2.0 / D * qrow_ss * support_images.astype(jnp.float32)
     return (total_sup * (summed + local_rows), loss_value)

time: 942 us -> 908 us (0.964)
  waiting for transfers between devices: 493 us -> 450 us
    psum x1 -> x0, waiting for transfers between devices: 42.1 us -> none  [body(): summed = lax.psum(partial_rows, 'tgt')]
  transfers between devices with their start and end apart: 5 -> 4, of which waited for: 5 -> 4; matrix products, arithmetic and copies ran while one was open for 14% -> 14% of each run, Pallas kernels for 0% -> 0%
where the time goes in v1:
time: 908 us; the launch traced here: 903 us
  waiting for transfers between devices  450 us (50%)
  other arithmetic  201 us (22%)
  matrix products  115 us (13%)
  blocking collectives  86.9 us (10%)
  local copies, waits for them, and re-layouts  30.2 us (3%)
  between operations  19.4 us (2%)
    reduce_scatter x1, waiting for transfers between devices, body(): lax.psum_scatter(term_rows(jnp.int32(0), sup_rows * lax.axis_size('sup'))...  175 us
    psum x1, waiting for transfers between devices, body(): d_coeffs, loss_value = lax.psum((d_coeff_part, loss_part), ('tgt', 'sup'))  158 us
    another operation x15, other arithmetic, body(): factor = jnp.linalg.cholesky(system)  82.1 us
    all_gather x1, waiting for transfers between devices, body(): gathered = lax.all_gather(support_images, 'sup', axis=0, tiled=True)  81.9 us
    psum x1, blocking collectives, body(): d_coeffs, loss_value = lax.psum((d_coeff_part, loss_part), ('tgt', 'sup'))  78.2 us
    reduce_sum x7, other arithmetic, ntk_kernel(): spread = (1.0 + 2.0 * norm_row) * (1.0 + 2.0 * norm_col)  44.2 us
    another operation x4, other arithmetic, ridge_solve(): lax.linalg.triangular_solve(factor, middle, left_side=True, lower=True, t...  43.1 us
    dot_general x1, matrix products, body(): lax.dot_general(target_images, gathered, contract, preferred_element_type...  37 us
  transfers between devices with their start and end apart: 4, of which 4 were waited for; matrix products, arithmetic and copies ran while one was open for 14% of the time, Pallas kernels for 0%

profile of v1, /device:TPU:1, one launch (start us, length us, event | category | flops | bytes accessed | tf_op | source)
XLA Modules:
  0.0 903.1 jit_solution(9569594725158152154)
XLA Ops:
  10.7 4.1 multiply_reduce_fusion
  15.9 81.9 %all-gather.4.cloned.1.call-done = bf16[512,3072]{1,0:T(8,128)(2,1)} async-done(((bf16[8,3072]{1,0:T(8,128)(2,1)}), bf16[512,3072]{1,0:T(8,128)(2,1)}) %all-gather.4.cloned.1.call-update) | async-done | bytes 3145744 | tf_op jit(solution)/shard_map/all_gather | solution.py:57
  97.8 2.7 fusion
  101.3 1.8 multiply_add_fusion.5
  103.5 37.0 %multiply_add_fusion = (f32[1024,512]{1,0:T(8,128)}, f32[1024,512]{1,0:T(8,128)}, f32[1024,512]{1,0:T(8,128)}, f32[1024,512]{1,0:T(8,128)}) fusion(f32[512]{0:T(512)S(1)} %get-tuple-element.154, f32[1024]{0:T(1024)S(1)} %multiply_add_fusion.10, f32[512]{0:T(512)S(1)} %get-tuple-element.119, f32[1024]{0:T(1024)S(1)} %get-tuple-element.135, ...), kind=kOutput, calls=%fused_computation.109 | convolution fusion | flops 3261071360 | bytes 17856512 | tf_op jit(solution)/shard_map/dot_general | solution.py:62
  140.5 35.2 %all-gather.6.cloned.1.call-done = f32[512,512]{1,0:T(8,128)} async-done(((f32[8,512]{1,0:T(8,128)}), f32[512,512]{1,0:T(8,128)}) %all-gather.6.cloned.1.call-update) | async-done | bytes 1048592 | tf_op jit(solution)/shard_map/all_gather | solution.py:69
  175.7 2.5 copy.23
  178.2 1.9 select_reduce_fusion
  180.8 2.3 select_add_fusion
  183.1 2.6 copy.24
  185.7 1.8 fusion.99
  187.5 1.1 copy-done.3
  188.6 11.7 %cholesky.103 = f32[128,128]{1,0:T(8,128)S(1)} custom-call(f32[128,128]{1,0:T(8,128)S(1)} %cholesky.263), custom_call_target="Cholesky" | custom-call | tf_op jit(solution)/shard_map/jit(cholesky)/cholesky | solution.py:72
  200.9 9.8 %custom-call.33 = f32[1,128,128]{1,2,0:T(8,128)S(1)} custom-call(f32[1,128,128]{2,1,0:T(8,128)S(1)} %get-tuple-element.131), custom_call_target="InvertDiagBlocksLowerTriangular" | custom-call | tf_op jit(solution)/shard_map/jit(cholesky)/cholesky | solution.py:72
  210.7 1.2 fusion.110
  212.0 1.3 convolution_subtract_fusion.1
  213.9 11.7 %cholesky.215 = f32[128,128]{1,0:T(8,128)S(1)} custom-call(f32[128,128]{1,0:T(8,128)S(1)} %cholesky.267), custom_call_target="Cholesky" | custom-call | tf_op jit(solution)/shard_map/jit(cholesky)/cholesky | solution.py:72
  225.7 1.2 select_reduce_fusion.3
  228.7 1.1 cholesky.222
  229.8 11.0 %custom-call.34 = f32[1,128,128]{1,2,0:T(8,128)S(1)} custom-call(f32[1,128,128]{2,1,0:T(8,128)} %get-tuple-element.129), custom_call_target="InvertDiagBlocksLowerTriangular" | custom-call | tf_op jit(solution)/shard_map/jit(cholesky)/cholesky | solution.py:72
  241.5 1.5 constant_dynamic-update-slice_fusion.2
  243.0 1.9 convolution_dynamic-update-slice_fusion
  244.9 1.6 convolution_subtract_fusion.2
  246.5 11.7 %cholesky.236 = f32[128,128]{1,0:T(8,128)S(1)} custom-call(f32[128,128]{1,0:T(8,128)S(1)} %cholesky.272), custom_call_target="Cholesky" | custom-call | tf_op jit(solution)/shard_map/jit(cholesky)/cholesky | solution.py:72
  259.0 9.8 %custom-call.35 = f32[1,128,128]{1,2,0:T(8,128)S(1)} custom-call(f32[1,128,128]{2,1,0:T(8,128)S(1)} %get-tuple-element.127), custom_call_target="InvertDiagBlocksLowerTriangular" | custom-call | tf_op jit(solution)/shard_map/jit(cholesky)/cholesky | solution.py:72
  269.7 1.5 convolution_subtract_fusion.6
  271.3 11.9 %cholesky.253 = f32[128,128]{1,0:T(8,128)S(1)} custom-call(f32[128,128]{1,0:T(8,128)S(1)} %convolution_subtract_fusion.6), custom_call_target="Cholesky" | custom-call | tf_op jit(solution)/shard_map/jit(cholesky)/cholesky | solution.py:72
  289.0 2.4 select_select_fusion
  291.4 14.8 %while.8 = (s32[]{:T(128)}, f32[512,512]{0,1:T(8,128)}, s32[4,2]{0,1:T(2,128)S(1)}, f32[4,128,128]{2,1,0:T(8,128)}, s32[]{:T(128)}) while((s32[]{:T(128)}, f32[512,512]{0,1:T(8,128)}, s32[4,2]{0,1:T(2,128)S(1)}, f32[4,128,128]{2,1,0:T(8,128)}, s32[]{:T(128)}) %tuple.98), condition=%wide.while_cond.1, body=%wide.while_body.1.sunk | while | flops 2 | bytes 393829 | solution.py:29
  292.1 2.3 dynamic-slice.14
  295.8 2.3 dynamic-slice.14
  299.6 2.3 dynamic-slice.14
  303.3 2.3 dynamic-slice.14
  306.3 40.1 %custom-call.39 = f32[4,128,128]{1,2,0:T(8,128)S(1)} custom-call(f32[4,128,128]{2,1,0:T(8,128)} %get-tuple-element.33), custom_call_target="InvertDiagBlocksLowerTriangular" | custom-call | tf_op jit(solution)/shard_map/triangular_solve/custom-call.8 | solution.py:29
  346.4 1.3 fusion.155
  347.7 1.2 convolution_subtract_fusion.4
  349.2 1.3 convolution_subtract_fusion.3
  350.8 1.4 convolution_subtract_fusion.5
  352.8 1.1 convolution_subtract_fusion.12
  354.1 1.2 convolution_subtract_fusion.11
  355.6 1.3 convolution_subtract_fusion.15
  357.2 2.8 multiply_reduce_fusion.1
  360.8 2.1 fusion.102
  363.1 18.7 %fusion.81 = (f32[1024,512]{1,0:T(8,128)S(1)}, f32[1024,512]{1,0:T(8,128)S(1)}, f32[1024,512]{1,0:T(8,128)S(1)}) fusion(f32[512]{0:T(512)} %copy-done.32, f32[1024]{0:T(1024)} %copy-done.50, f32[512]{0:T(512)S(1)} %copy-done.20, f32[1024]{0:T(1024)} %copy-done.38, f32[1024,512]{1,0:T(8,128)} %get-tuple-element.115, f32[512]{0:T(512)S(1)} %copy-done.22, ...), kind=kOutput, calls=%fused_computation.97 | convolution fusion | flops 658761728 | bytes 11118592 | tf_op jit(solution)/shard_map/dot_general | solution.py:92
  381.9 26.9 %fusion.92 = (f32[512]{0:T(512)}, f32[512]{0:T(512)}, f32[512]{0:T(512)}, f32[1024,512]{1,0:T(8,128)S(1)}, f32[1024,512]{1,0:T(8,128)S(1)}) fusion(f32[512]{0:T(512)S(1)} %copy-done.33, f32[1024]{0:T(1024)S(1)} %copy-done.51, f32[1024,512]{1,0:T(8,128)S(1)} %get-tuple-element.151, f32[1024,512]{1,0:T(8,128)S(1)} %copy-done.58, f32[512]{0:T(512)S(1)} %copy-done.20, ...), kind=kLoop, calls=%fused_computation.128 | loop fusion | flops 67107328 | bytes 16814080 | tf_op jit(solution)/shard_map/transpose(jvp())/reduce_sum | solution.py:17
  408.8 14.4 %fusion.61 = (f32[1024,512]{1,0:T(8,128)S(1)}, f32[1024,512]{1,0:T(8,128)S(1)}) fusion(f32[1024,512]{1,0:T(8,128)S(1)} %get-tuple-element.92, f32[1024,512]{1,0:T(8,128)S(1)} %get-tuple-element.91, f32[1024,512]{1,0:T(8,128)S(1)} %copy-done.4, f32[512]{0:T(512)S(1)} %copy-done.22, f32[1024]{0:T(1024)S(1)} %copy-done.37, f32[512]{0:T(512)S(1)} %copy-done.17, ...), kind=kLoop, calls=%fused_computation.77 | loop fusion | flops 24117248 | bytes 14704640 | tf_op jit(solution)/shard_map/transpose(jvp())/mul | solution.py:18
  423.2 12.5 %fusion.89 = (f32[512]{0:T(512)}, f32[512]{0:T(512)}, f32[1024,512]{1,0:T(8,128)S(1)}) fusion(f32[1024,512]{1,0:T(8,128)S(1)} %get-tuple-element.103, f32[512]{0:T(512)S(1)} %copy-done.17, f32[1024]{0:T(1024)S(1)} %copy-done.26, f32[1024,512]{1,0:T(8,128)S(1)} %get-tuple-element.104, f32[1024,512]{1,0:T(8,128)S(1)} %copy-done.2, f32[512]{0:T(512)S(1)} %copy-done.15, ...), kind=kLoop, calls=%fused_computation.125 | loop fusion | flops 36699136 | bytes 8404992 | tf_op jit(solution)/shard_map/transpose(jvp())/reduce_sum | solution.py:17
  435.6 14.1 %fusion.100 = f32[512,3072]{1,0:T(8,128)} fusion(bf16[1024,3072]{1,0:T(8,128)(2,1)S(1)} %bitcast.105, f32[1024,512]{1,0:T(8,128)S(1)} %get-tuple-element.93, f32[1024,512]{1,0:T(8,128)S(1)} %copy-done.2, f32[512]{0:T(512)S(1)} %copy-done.15, f32[1024]{0:T(1024)S(1)} %copy-done.24, f32[1024,512]{1,0:T(8,128)S(1)} %get-tuple-element.104, ...), kind=kOutput, calls=%fused_computation.161 | convolution fusion | flops 3242196992 | bytes 18886656 | tf_op jit(solution)/shard_map/dot_general | solution.py:38
  449.7 157.8 %all-reduce.3.cloned.1.call-done = f32[512,100]{0,1:T(8,128)} async-done(((f32[512,100]{0,1:T(8,128)}), f32[512,100]{0,1:T(8,128)}) %all-reduce.3.cloned.1.call-update) | async-done | bytes 204816 | tf_op jit(solution)/shard_map/psum | solution.py:81
  607.5 1.1 fusion.166
  608.6 1.1 convolution_subtract_fusion.10
  609.9 1.2 convolution_subtract_fusion.9
  611.5 1.3 convolution_subtract_fusion.14
  613.3 1.1 convolution_subtract_fusion.8
  614.7 1.2 convolution_subtract_fusion.7
  616.1 1.3 convolution_subtract_fusion.13
  619.0 1.3 fusion.209
  620.2 1.1 multiply_reduce_fusion.6
  621.3 1.1 multiply_reduce_fusion.5
  625.9 6.9 fusion.1
  633.6 78.2 %psum.15 = f32[]{:T(128)} all-reduce(f32[]{:T(128)S(6)} %div.757), channel_id=1, replica_groups=mesh['tgt'=4,'sup'=64] {'tgt','sup'}, use_global_device_ids=true, to_apply=%region_32.35 | all-reduce | flops 1 | bytes 8 | tf_op jit(solution)/shard_map/psum | solution.py:81
  711.8 174.5 %reduce-scatter.2.cloned.1.call-done = f32[8,3072]{1,0:T(8,128)} async-done(((f32[512,3072]{1,0:T(8,128)}), f32[8,3072]{1,0:T(8,128)}) %reduce-scatter.2.cloned.1.call-update) | async-done | bytes 98320 | tf_op jit(solution)/shard_map/reduce_scatter | solution.py:102
  886.3 8.7 all-gather
  895.1 1.3 fusion.3
  (199 shorter events, 28.9 us)
Async XLA Ops:
  7.2 90.6 %all-gather.4.cloned.1.call-start = ((), (), s32[]{:S(2)}) async-start(), calls=%async_computation.1 | async-start | bytes 3194880 | tf_op jit(solution)/shard_map/all_gather | solution.py:57
  7.9 167.8 %all-gather.6.cloned.1.call-start = ((), (), s32[]{:S(2)}) async-start(), calls=%async_computation.2 | async-start | bytes 1064960 | tf_op jit(solution)/shard_map/all_gather | solution.py:69
  10.1 0.6 copy-start.44
  10.1 0.6 copy-start.46
  10.1 4.7 copy-start.53
  10.1 91.2 %copy-start.27 = (f32[8]{0:T(128)}, f32[8]{0:T(128)S(1)}, u32[]{:S(2)}) copy-start(f32[8]{0:T(128)S(1)} %get-tuple-element.148) | copy-start | bytes 100
  10.2 91.2 %copy-start.40 = (f32[8]{0:T(128)}, f32[8]{0:T(128)S(1)}, u32[]{:S(2)}) copy-start(f32[8]{0:T(128)S(1)} %get-tuple-element.110) | copy-start | bytes 100
  10.2 91.1 %copy-start.34 = (f32[8]{0:T(128)}, f32[8]{0:T(128)S(1)}, u32[]{:S(2)}) copy-start(f32[8]{0:T(128)S(1)} %broadcast_add_fusion.8) | copy-start | bytes 100
  10.7 90.6 %copy-start.41 = (f32[8]{0:T(128)}, f32[8]{0:T(128)S(1)}, u32[]{:S(2)}) copy-start(f32[8]{0:T(128)S(1)} %get-tuple-element.156) | copy-start | bytes 100
  10.7 90.6 %copy-start.48 = (f32[8]{0:T(128)}, f32[8]{0:T(128)S(1)}, u32[]{:S(2)}) copy-start(f32[8]{0:T(128)S(1)} %get-tuple-element.155) | copy-start | bytes 100
  10.7 4.4 copy-start.52
  14.8 86.5 %copy-start.6 = (bf16[8,3072]{1,0:T(8,128)(2,1)S(1)}, bf16[8,3072]{1,0:T(8,128)(2,1)}, u32[]{:S(2)}) copy-start(bf16[8,3072]{1,0:T(8,128)(2,1)} %param.8) | copy-start | bytes 147460
  15.0 88.4 %copy-start.23 = (f32[1024]{0:T(1024)}, f32[1024]{0:T(1024)S(1)}, u32[]{:S(2)}) copy-start(f32[1024]{0:T(1024)S(1)} %get-tuple-element.133) | copy-start | bytes 12292
  15.0 88.4 %copy-start.25 = (f32[1024]{0:T(1024)}, f32[1024]{0:T(1024)S(1)}, u32[]{:S(2)}) copy-start(f32[1024]{0:T(1024)S(1)} %get-tuple-element.137) | copy-start | bytes 12292
  15.0 88.4 %copy-start.36 = (f32[1024]{0:T(1024)}, f32[1024]{0:T(1024)S(1)}, u32[]{:S(2)}) copy-start(f32[1024]{0:T(1024)S(1)} %get-tuple-element.134) | copy-start | bytes 12292
  15.0 88.4 %copy-start.38 = (f32[1024]{0:T(1024)}, f32[1024]{0:T(1024)S(1)}, u32[]{:S(2)}) copy-start(f32[1024]{0:T(1024)S(1)} %get-tuple-element.135) | copy-start | bytes 12292
  15.1 88.4 %copy-start.50 = (f32[1024]{0:T(1024)}, f32[1024]{0:T(1024)S(1)}, u32[]{:S(2)}) copy-start(f32[1024]{0:T(1024)S(1)} %multiply_add_fusion.10) | copy-start | bytes 12292
  97.8 3.5 copy-start
  100.5 0.6 copy-start.31
  100.7 0.5 copy-start.29
  100.7 0.6 copy-start.30
  100.7 39.7 %copy-start.14 = (f32[512]{0:T(512)}, f32[512]{0:T(512)S(1)}, u32[]{:S(2)}) copy-start(f32[512]{0:T(512)S(1)} %get-tuple-element.145) | copy-start | bytes 6148
  100.7 39.7 %copy-start.19 = (f32[512]{0:T(512)}, f32[512]{0:T(512)S(1)}, u32[]{:S(2)}) copy-start(f32[512]{0:T(512)S(1)} %get-tuple-element.119) | copy-start | bytes 6148
  101.2 39.3 %copy-start.16 = (f32[512]{0:T(512)}, f32[512]{0:T(512)S(1)}, u32[]{:S(2)}) copy-start(f32[512]{0:T(512)S(1)} %get-tuple-element.146) | copy-start | bytes 6148
  101.2 39.3 %copy-start.21 = (f32[512]{0:T(512)}, f32[512]{0:T(512)S(1)}, u32[]{:S(2)}) copy-start(f32[512]{0:T(512)S(1)} %get-tuple-element.147) | copy-start | bytes 6148
  101.2 39.3 %copy-start.32 = (f32[512]{0:T(512)}, f32[512]{0:T(512)S(1)}, u32[]{:S(2)}) copy-start(f32[512]{0:T(512)S(1)} %get-tuple-element.154) | copy-start | bytes 6148
  103.2 504.3 %all-reduce.3.cloned.1.call-start = ((), (), s32[]{:S(2)}) async-start(), calls=%async_computation.3 | async-start | bytes 425984 | tf_op jit(solution)/shard_map/psum | solution.py:81
  187.5 1.1 copy-start.3
  200.3 0.6 copy-start.13
  213.2 0.7 copy-start.10
  241.5 41.8 %copy-start.56 = (f32[128]{0:T(128)S(1)}, f32[128]{0:T(128)}, u32[]{:S(2)}) copy-start(f32[128]{0:T(128)} %get-tuple-element.128) | copy-start | bytes 1540
  241.5 42.4 %copy-start.55 = (f32[128]{0:T(128)S(1)}, f32[128]{0:T(128)}, u32[]{:S(2)}) copy-start(f32[128]{0:T(128)} %get-tuple-element.130) | copy-start | bytes 1540
  244.8 46.6 %copy-start.57 = (s32[4]{0:T(128)S(1)}, s32[4]{0:T(128)}, u32[]{:S(2)}) copy-start(s32[4]{0:T(128)} %iota_multiply_fusion) | copy-start | bytes 52
  306.3 50.9 %copy-start.49 = (s32[1024]{0:T(1024)S(1)}, s32[1024]{0:T(1024)}, u32[]{:S(2)}) copy-start(s32[1024]{0:T(1024)} %param.11) | copy-start | bytes 12292
  346.4 10.8 %copy-start.1 = (f32[1024,512]{1,0:T(8,128)S(1)}, f32[1024,512]{1,0:T(8,128)}, u32[]{:S(2)}) copy-start(f32[1024,512]{1,0:T(8,128)} %get-tuple-element.114) | copy-start | bytes 6291460
  355.6 1.6 copy-start.8
  357.1 2.9 copy-start.11
  360.0 0.8 copy-start.5
  360.0 2.9 copy-start.20
  360.0 2.9 copy-start.22
  362.9 523.4 %reduce-scatter.2.cloned.1.call-start = ((), (), s32[]{:S(2)}) async-start(), calls=%async_computation.4 | async-start | bytes 6389760 | tf_op jit(solution)/shard_map/reduce_scatter | solution.py:102
  362.9 18.8 %copy-start.2 = (f32[1024,512]{1,0:T(8,128)S(1)}, f32[1024,512]{1,0:T(8,128)}, u32[]{:S(2)}) copy-start(f32[1024,512]{1,0:T(8,128)} %get-tuple-element.149) | copy-start | bytes 6291460
  363.0 18.8 %copy-start.4 = (f32[1024,512]{1,0:T(8,128)S(1)}, f32[1024,512]{1,0:T(8,128)}, u32[]{:S(2)}) copy-start(f32[1024,512]{1,0:T(8,128)} %get-tuple-element.116) | copy-start | bytes 6291460
  363.0 18.8 %copy-start.15 = (f32[512]{0:T(512)S(1)}, f32[512]{0:T(512)}, u32[]{:S(2)}) copy-start(f32[512]{0:T(512)} %copy-done.14) | copy-start | bytes 6148
  363.0 18.8 %copy-start.17 = (f32[512]{0:T(512)S(1)}, f32[512]{0:T(512)}, u32[]{:S(2)}) copy-start(f32[512]{0:T(512)} %copy-done.16) | copy-start | bytes 6148
  363.0 18.8 %copy-start.24 = (f32[1024]{0:T(1024)S(1)}, f32[1024]{0:T(1024)}, u32[]{:S(2)}) copy-start(f32[1024]{0:T(1024)} %copy-done.23) | copy-start | bytes 12292
  363.0 18.8 %copy-start.26 = (f32[1024]{0:T(1024)S(1)}, f32[1024]{0:T(1024)}, u32[]{:S(2)}) copy-start(f32[1024]{0:T(1024)} %copy-done.25) | copy-start | bytes 12292
  363.0 18.8 %copy-start.33 = (f32[512]{0:T(512)S(1)}, f32[512]{0:T(512)}, u32[]{:S(2)}) copy-start(f32[512]{0:T(512)} %copy-done.32) | copy-start | bytes 6148
  363.0 18.8 %copy-start.37 = (f32[1024]{0:T(1024)S(1)}, f32[1024]{0:T(1024)}, u32[]{:S(2)}) copy-start(f32[1024]{0:T(1024)} %copy-done.36) | copy-start | bytes 12292
  363.0 18.8 %copy-start.39 = (f32[1024]{0:T(1024)S(1)}, f32[1024]{0:T(1024)}, u32[]{:S(2)}) copy-start(f32[1024]{0:T(1024)} %copy-done.38) | copy-start | bytes 12292
  363.0 18.8 %copy-start.51 = (f32[1024]{0:T(1024)S(1)}, f32[1024]{0:T(1024)}, u32[]{:S(2)}) copy-start(f32[1024]{0:T(1024)} %copy-done.50) | copy-start | bytes 12292
  363.0 18.8 %copy-start.58 = (f32[1024,512]{1,0:T(8,128)S(1)}, f32[1024,512]{1,0:T(8,128)}, u32[]{:S(2)}) copy-start(f32[1024,512]{1,0:T(8,128)} %get-tuple-element.115) | copy-start | bytes 6291460
  381.9 53.8 %slice-start = ((s8[6291456]{0:T(1024)(128)(4,1)}), s8[4194304]{0:T(1024)(128)(4,1)S(1)}, s32[]{:S(2)}) async-start(s8[6291456]{0:T(1024)(128)(4,1)} %bitcast.104), calls=%async_computation.5 | async-start | bytes 8388608
  408.8 26.9 %slice-start.1 = ((s8[6291456]{0:T(1024)(128)(4,1)}), s8[2097152]{0:T(1024)(128)(4,1)S(1)}, s32[]{:S(2)}) async-start(s8[6291456]{0:T(1024)(128)(4,1)} %bitcast.104), calls=%async_computation.6 | async-start | bytes 4194304
  449.7 169.3 %copy-start.18 = (f32[8,512]{1,0:T(8,128)S(1)}, f32[8,512]{1,0:T(8,128)}, u32[]{:S(2)}) copy-start(f32[8,512]{1,0:T(8,128)} %get-tuple-element.109) | copy-start | bytes 49156
  607.5 10.2 %copy-start.9 = (f32[128,100]{0,1:T(8,128)S(1)}, f32[128,100]{0,1:T(8,128)}, u32[]{:S(2)}) copy-start(f32[128,100]{0,1:T(8,128)} %copy-done.8) | copy-start | bytes 153604
  607.5 10.2 %copy-start.12 = (f32[128,100]{0,1:T(8,128)S(1)}, f32[128,100]{0,1:T(8,128)}, u32[]{:S(2)}) copy-start(f32[128,100]{0,1:T(8,128)} %copy-done.11) | copy-start | bytes 153604
  632.8 78.9 %copy-start.43 = (f32[8]{0:T(128)S(1)}, f32[8]{0:T(128)}, u32[]{:S(2)}) copy-start(f32[8]{0:T(128)} %copy-done.42) | copy-start | bytes 100
  632.8 78.9 %copy-start.45 = (f32[8]{0:T(128)S(1)}, f32[8]{0:T(128)}, u32[]{:S(2)}) copy-start(f32[8]{0:T(128)} %copy-done.44) | copy-start | bytes 100
  632.8 78.9 %copy-start.47 = (f32[8]{0:T(128)S(1)}, f32[8]{0:T(128)}, u32[]{:S(2)}) copy-start(f32[8]{0:T(128)} %copy-done.46) | copy-start | bytes 100
  632.8 78.9 %copy-start.54 = (f32[8]{0:T(128)S(1)}, f32[8]{0:T(128)}, u32[]{:S(2)}) copy-start(f32[8]{0:T(128)} %copy-done.53) | copy-start | bytes 100
  632.8 262.2 %copy-start.7 = (bf16[8,3072]{1,0:T(8,128)(2,1)S(1)}, bf16[8,3072]{1,0:T(8,128)(2,1)}, u32[]{:S(2)}) copy-start(bf16[8,3072]{1,0:T(8,128)(2,1)} %param.8) | copy-start | bytes 147460
  632.9 262.2 %copy-start.28 = (f32[8]{0:T(128)S(1)}, f32[8]{0:T(128)}, u32[]{:S(2)}) copy-start(f32[8]{0:T(128)} %copy-done.27) | copy-start | bytes 100
  632.9 262.2 %copy-start.35 = (f32[8]{0:T(128)S(1)}, f32[8]{0:T(128)}, u32[]{:S(2)}) copy-start(f32[8]{0:T(128)} %copy-done.34) | copy-start | bytes 100
  (1 other events, 0.5 us)
Sparse Core Ops, SparseCore 0:
  11.3 86.4 all-gather.3
  103.3 72.3 all-gather.5
  363.0 244.4 all-reduce.2
  633.0 253.2 reduce-scatter.1
